TPU v7x, 256 devices: a whole 4x4x8 slice. The times are simulated.
256 devices in a mesh: row: 32 (over y, z), col: 8 (over x, core).
Axes of the slice: x: 4, y: 4, z: 8, core: 2. Of those that a mesh axis runs over, the one named last changes fastest.
Arguments:
- points: float32 [65536, 16], P(('row', 'col')), may hold values from -6 to 6
- inv_lengths: float32 [16], replicated, may hold values from 0.35 to 0.7
- signal_level: float32 [1], replicated, may hold values from 0.5 to 2
- noise_level: float32 [1], replicated, may hold values from 0.05 to 0.5
- right_sides: float32 [65536, 32], P(('row', 'col')), may hold values from -6 to 6
- block_counts: int32 [256], P(('row', 'col')), may hold values from 1 to 256, 49152 in all
Outputs:
- solution: float32 [65536, 32], P(('row', 'col'))
- residual: float32 [65536, 32], P(('row', 'col'))
Inputs may be any that keep to these rules, and one draw needn't show every extreme that they name: `block_counts`: each block of 256 slots holds its valid points first; the slots after them are padding.
All inputs are finite; a program needn't handle non-finite values.
Results may differ from a plain program's by a relative error of at most 0.012.
The roundings to bfloat16 on the way count: a program that leaves them out, or rounds other values in their place, can miss the bound.
Values may be sent and summed in bfloat16 or wider, within the bound.
A program may use at most 64 MiB of HBM per device.

v0:
```python
import math
import jax
import jax.numpy as jnp
from jax import lax
from jax.sharding import PartitionSpec as P

ITERS = 2


def kernel_tile(scaled_rows, square_rows, scaled_cols, square_cols, signal):
    inner_product = lax.dot_general(
        scaled_rows,
        scaled_cols,
        (((1,), (1,)), ((), ())),
        precision=lax.Precision.HIGHEST,
        preferred_element_type=jnp.float32,
    )
    distance = square_rows[:, None] + square_cols[None, :] - 2.0 * inner_product
    return (signal * jnp.exp(-0.5 * distance)).astype(jnp.bfloat16)


def column_norm(residual):
    return lax.psum(jnp.sum(residual * residual, axis=0), ("row", "col"))


def column_sweep(scaled_rows, square_rows, scaled_cols, square_cols, direction, signal):
    feat_count = scaled_rows.shape[1]
    zero_rows = jnp.zeros((scaled_rows.shape[0], direction.shape[1]), jnp.float32)
    running = zero_rows
    piece = lax.all_gather(direction, "row", axis=0, tiled=True)
    piece_rows = piece.shape[0]
    sub_rows = math.gcd(piece_rows, 512)
    pieces_count = piece_rows // sub_rows

    def advance(carried, parts):
        scaled_part, square_part, dir_part = parts
        kernel_block = kernel_tile(scaled_rows, square_rows, scaled_part, square_part, signal)
        return (carried + jnp.dot(kernel_block, dir_part, preferred_element_type=jnp.float32), None)

    running, unused = lax.scan(
        advance,
        running,
        (
            scaled_cols.reshape(pieces_count, sub_rows, feat_count),
            square_cols.reshape(pieces_count, sub_rows),
            piece.reshape(pieces_count, sub_rows, piece.shape[1]),
        ),
    )
    return running


def body(points, inv_lengths, signal_level, noise_level, right_sides, block_counts):
    block_rows = points.shape[0]
    signal = signal_level[0]
    noise_var = noise_level[0]
    scaled_own = points * inv_lengths[None, :]
    scaled_rows = lax.all_gather(scaled_own, "col", axis=0, tiled=True)
    square_rows = jnp.sum(scaled_rows * scaled_rows, axis=1)
    scaled_cols = lax.all_gather(scaled_own, "row", axis=0, tiled=True)
    square_cols = jnp.sum(scaled_cols * scaled_cols, axis=1)
    slots = jnp.arange(block_rows, dtype=jnp.int32)
    valid_rows = (slots < block_counts[0]).astype(jnp.float32)[:, None]
    residual = valid_rows * right_sides
    solution = jnp.zeros_like(residual)
    direction = residual.astype(jnp.bfloat16)
    norm_now = column_norm(residual)
    for iteration in range(ITERS):
        dir_float = direction.astype(jnp.float32)
        forward = column_sweep(
            scaled_rows, square_rows, scaled_cols, square_cols, direction, signal
        )
        reduced = lax.psum_scatter(forward, "col", scatter_dimension=0, tiled=True)
        applied = valid_rows * reduced + noise_var * dir_float
        curvature = lax.psum(jnp.sum(dir_float * applied, axis=0), ("row", "col"))
        applied, curvature = (applied, curvature)
        dir_float = direction.astype(jnp.float32)
        step_size = norm_now / curvature
        solution = solution + step_size * dir_float
        residual = residual - step_size * applied
        if iteration + 1 < ITERS:
            norm_next = column_norm(residual)
            direction = (residual + norm_next / norm_now * dir_float).astype(jnp.bfloat16)
            norm_now = norm_next
    return (solution, residual)


def solution(mesh):
    in_specs = (P(("row", "col"), None), P(), P(), P(), P(("row", "col"), None), P(("row", "col")))
    out_specs = (P(("row", "col"), None), P(("row", "col"), None))
    return jax.shard_map(body, mesh=mesh, in_specs=in_specs, out_specs=out_specs, check_vma=False)
```

profile of v0, /device:TPU:1, one launch (start us, length us, event | category | flops | bytes accessed | tf_op | source)
XLA Modules:
  0.0 683.2 jit_solution(8978833498880750130)
XLA Ops:
  8.0 15.8 %all_gather.12 = f32[2048,16]{0,1:T(8,128)S(1)} all-gather(f32[256,16]{0,1:T(8,128)S(1)} %broadcast_multiply_fusion), channel_id=1, replica_groups=mesh['row'=32,'col'=8] {'col'}, dimensions={0}, use_global_device_ids=true | all-gather | bytes 147456 | tf_op jit(solution)/shard_map/all_gather | solution.py:57
  23.8 39.8 %all_gather.13 = f32[8192,16]{0,1:T(8,128)S(1)} all-gather(f32[256,16]{0,1:T(8,128)S(1)} %broadcast_multiply_fusion), channel_id=1, replica_groups=mesh['row'=32,'col'=8] {'row'}, dimensions={0}, use_global_device_ids=true | all-gather | bytes 540672 | tf_op jit(solution)/shard_map/all_gather | solution.py:59
  65.0 32.2 %all_gather.14 = bf16[8192,32]{0,1:T(8,128)(2,1)S(1)} all-gather(bf16[256,32]{0,1:T(8,128)(2,1)S(1)} %multiply_convert_fusion), channel_id=1, replica_groups=mesh['row'=32,'col'=8] {'row'}, dimensions={0}, use_global_device_ids=true | all-gather | bytes 540672 | tf_op jit(solution)/shard_map/all_gather | solution.py:30
  99.3 109.9 %while.22 = (s32[]{:T(128)}, f32[2048,32]{0,1:T(8,128)S(1)}, f32[]{:T(128)}, f32[2048]{0:T(1024)S(1)}, f32[16,512]{1,0:T(8,128)S(1)}, /*index=5*/f32[16,512,16]{...) while((s32[]{:T(128)}, f32[2048,32]{0,1:T(8,128)S(1)}, ...), condition=%wide.region_5.6_spmd.clone, body=%wide.region_4.5_spmd.clone.sunk | while | flops 274857984 | bytes 5028475 | solution.py:40
  210.6 48.9 %reduce-scatter.3.cloned.1.call-done = f32[256,32]{0,1:T(8,128)} async-done(((f32[2048,32]{0,1:T(8,128)}), f32[256,32]{0,1:T(8,128)}) %reduce-scatter.3.cloned.1.call-update) | async-done | bytes 32784 | tf_op jit(solution)/shard_map/reduce_scatter | solution.py:72
  260.4 78.2 %all-reduce = (f32[32]{0:T(128)S(1)}, f32[32]{0:T(128)S(1)}) all-reduce(f32[32]{0:T(128)S(1)} %get-tuple-element.175, f32[32]{0:T(128)S(1)} %get-tuple-element.174), channel_id=1, replica_groups=mesh['row'=32,'col'=8] {'row','col'}, use_global_device_ids=true, to_apply=%region_1.0 | all-reduce | flops 64 | bytes 512 | tf_op jit(solution)/shard_map/psum | solution.py:23
  339.6 73.1 %psum.30 = f32[32]{0:T(128)S(1)} all-reduce(f32[32]{0:T(128)S(1)} %get-tuple-element.210), channel_id=1, replica_groups=mesh['row'=32,'col'=8] {'row','col'}, use_global_device_ids=true, to_apply=%region_10.11 | all-reduce | flops 32 | bytes 256 | tf_op jit(solution)/shard_map/psum | solution.py:23
  412.7 33.5 %all_gather.15 = bf16[8192,32]{0,1:T(8,128)(2,1)S(1)} all-gather(bf16[256,32]{0,1:T(8,128)(2,1)S(1)} %fusion.26), channel_id=1, replica_groups=mesh['row'=32,'col'=8] {'row'}, dimensions={0}, use_global_device_ids=true | all-gather | bytes 540672 | tf_op jit(solution)/shard_map/all_gather | solution.py:30
  448.0 110.0 %while.23 = (s32[]{:T(128)}, f32[2048,32]{0,1:T(8,128)S(1)}, f32[]{:T(128)}, f32[2048]{0:T(1024)S(1)}, f32[16,512]{1,0:T(8,128)S(1)}, /*index=5*/f32[16,512,16]{...) while((s32[]{:T(128)}, f32[2048,32]{0,1:T(8,128)S(1)}, ...), condition=%wide.region_12.13_spmd.clone, body=%wide.region_11.12_spmd.clone.sunk | while | flops 274857984 | bytes 5028475 | solution.py:40
  454.9 5.2 fusion.50
  461.8 5.2 fusion.50
  468.7 5.2 fusion.50
  475.5 5.2 fusion.50
  482.4 5.2 fusion.50
  489.3 5.2 fusion.50
  496.2 5.2 fusion.50
  503.0 5.2 fusion.50
  509.9 5.2 fusion.50
  516.8 5.2 fusion.50
  523.7 5.2 fusion.50
  537.4 5.2 fusion.50
  551.2 5.2 fusion.50
  558.7 37.0 %reduce-scatter.5.cloned.1.call-done = f32[256,32]{0,1:T(8,128)} async-done(((f32[2048,32]{0,1:T(8,128)}), f32[256,32]{0,1:T(8,128)}) %reduce-scatter.5.cloned.1.call-update) | async-done | bytes 32784 | tf_op jit(solution)/shard_map/reduce_scatter | solution.py:72
  596.6 78.2 %psum.31 = f32[32]{0:T(128)S(1)} all-reduce(f32[32]{0:T(128)S(1)} %fusion.21), channel_id=1, replica_groups=mesh['row'=32,'col'=8] {'row','col'}, use_global_device_ids=true, to_apply=%region_15.16 | all-reduce | flops 32 | bytes 256 | tf_op jit(solution)/shard_map/psum | solution.py:74
  (112 shorter events, 162.0 us)
Async XLA Ops:
  7.2 252.3 %reduce-scatter.3.cloned.1.call-start = ((), (), s32[]{:S(2)}) async-start(), calls=%async_computation.2 | async-start | bytes 294912 | tf_op jit(solution)/shard_map/reduce_scatter | solution.py:72
  99.2 160.3 %copy-start.2 = (f32[256,32]{0,1:T(8,128)S(1)}, f32[256,32]{0,1:T(8,128)}, u32[]{:S(2)}) copy-start(f32[256,32]{0,1:T(8,128)} %param.14) | copy-start | bytes 98308
  209.2 0.7 copy-start.1
  209.9 385.8 %reduce-scatter.5.cloned.1.call-start = ((), (), s32[]{:S(2)}) async-start(), calls=%async_computation.3 | async-start | bytes 294912 | tf_op jit(solution)/shard_map/reduce_scatter | solution.py:72
  558.0 0.7 copy-start
Sparse Core Ops, SparseCore 0:
  210.0 49.4 reduce-scatter.2
  558.8 36.8 reduce-scatter.4
where the time goes:
time: 685 us; the launch traced here: 683 us
  blocking collectives  351 us (51%)
  matrix products  218 us (32%)
  waiting for transfers between devices  85.9 us (13%)
  between operations  15.4 us (2%)
    dot_general x32, matrix products, kernel_tile(): lax.dot_general(scaled_rows, scaled_cols, (((1,), (1,)), ((), ())), preci...  166 us
    psum x2, blocking collectives, column_norm(): return lax.psum(jnp.sum(residual * residual, axis=0), ('row', 'col'))  151 us
    reduce_scatter x2, waiting for transfers between devices, body(): reduced = lax.psum_scatter(forward, 'col', scatter_dimension=0, tiled=True)  85.9 us
    psum x1, blocking collectives, body(): curvature = lax.psum(jnp.sum(dir_float * applied, axis=0), ('row', 'col'))  78.2 us
    all_gather x2, blocking collectives, column_sweep(): piece = lax.all_gather(direction, 'row', axis=0, tiled=True)  65.7 us
    dot_general x32, matrix products, advance(): jnp.dot(kernel_block, dir_part, preferred_element_type=jnp.float32)  52.1 us
    all_gather x1, blocking collectives, body(): scaled_cols = lax.all_gather(scaled_own, 'row', axis=0, tiled=True)  39.8 us
    all_gather x1, blocking collectives, body(): scaled_rows = lax.all_gather(scaled_own, 'col', axis=0, tiled=True)  15.8 us
  transfers between devices with their start and end apart: 2, of which 2 were waited for; matrix products, arithmetic and copies ran while one was open for 0% of the time, Pallas kernels for 0%

commit v1 on v0

--- a/solution.py
+++ b/solution.py
@@ -1,3 +1,4 @@
+import functools
 import math
 import jax
 import jax.numpy as jnp
@@ -5,6 +6,16 @@
 from jax.sharding import PartitionSpec as P
 
 ITERS = 2
+
+
+def trees_create(arr, mesh_ax):
+    upper = jnp.concatenate(
+        lax.all_to_all(jnp.stack([arr] * lax.axis_size(mesh_ax)), mesh_ax, 0, 0), 0
+    )
+    return upper
+
+
+form_gates = functools.partial(trees_create, mesh_ax="row")
 
 
 def kernel_tile(scaled_rows, square_rows, scaled_cols, square_cols, signal):
@@ -56,7 +67,7 @@
     scaled_own = points * inv_lengths[None, :]
     scaled_rows = lax.all_gather(scaled_own, "col", axis=0, tiled=True)
     square_rows = jnp.sum(scaled_rows * scaled_rows, axis=1)
-    scaled_cols = lax.all_gather(scaled_own, "row", axis=0, tiled=True)
+    scaled_cols = form_gates(scaled_own)
     square_cols = jnp.sum(scaled_cols * scaled_cols, axis=1)
     slots = jnp.arange(block_rows, dtype=jnp.int32)
     valid_rows = (slots < block_counts[0]).astype(jnp.float32)[:, None]

time: 685 us -> 649 us (0.947)
  blocking collectives: 351 us -> 325 us
  waiting for transfers between devices: 85.9 us -> 66.3 us
  starting transfers between devices: 0.08 us -> 12.1 us
    all_gather x1 -> x0, blocking collectives: 39.8 us -> none  [body(): scaled_cols = lax.all_gather(scaled_own, 'row', axis=0, tiled=True)]
    reduce_scatter x2, waiting for transfers between devices: 85.9 us -> 66.3 us  [body(): reduced = lax.psum_scatter(forward, 'col', scatter_dimension=0, tiled=True)]
    all_to_all x0 -> x1, starting transfers between devices: none -> 12 us  [trees_create(): lax.all_to_all(jnp.stack([arr] * lax.axis_size(mesh_ax)), mesh_ax, 0, 0)]
    all_gather x2, blocking collectives: 65.7 us -> 72.9 us  [column_sweep(): piece = lax.all_gather(direction, 'row', axis=0, tiled=True)]
    dot_general x32, matrix products: 52.1 us -> 45.1 us  [advance(): jnp.dot(kernel_block, dir_part, preferred_element_type=jnp.float32)]
  transfers between devices with their start and end apart: 2 -> 3, of which waited for: 2 -> 2; matrix products, arithmetic and copies ran while one was open for 0% -> 0% of each run, Pallas kernels for 0% -> 0%
where the time goes in v1:
time: 649 us; the launch traced here: 647 us
  blocking collectives  325 us (50%)
  matrix products  214 us (33%)
  waiting for transfers between devices  66.3 us (10%)
  between operations  15.5 us (2%)
  starting transfers between devices  12.1 us (2%)
  local copies, waits for them, and re-layouts  6.9 us (1%)
    dot_general x32, matrix products, kernel_tile(): lax.dot_general(scaled_rows, scaled_cols, (((1,), (1,)), ((), ())), preci...  169 us
    psum x2, blocking collectives, column_norm(): return lax.psum(jnp.sum(residual * residual, axis=0), ('row', 'col'))  151 us
    psum x1, blocking collectives, body(): curvature = lax.psum(jnp.sum(dir_float * applied, axis=0), ('row', 'col'))  78.2 us
    all_gather x2, blocking collectives, column_sweep(): piece = lax.all_gather(direction, 'row', axis=0, tiled=True)  72.9 us
    reduce_scatter x2, waiting for transfers between devices, body(): reduced = lax.psum_scatter(forward, 'col', scatter_dimension=0, tiled=True)  66.3 us
    dot_general x32, matrix products, advance(): jnp.dot(kernel_block, dir_part, preferred_element_type=jnp.float32)  45.1 us
    all_gather x1, blocking collectives, body(): scaled_rows = lax.all_gather(scaled_own, 'col', axis=0, tiled=True)  22.6 us
  transfers between devices with their start and end apart: 3, of which 2 were waited for; matrix products, arithmetic and copies ran while one was open for 0% of the time, Pallas kernels for 0%

profile of v1, /device:TPU:1, one launch (start us, length us, event | category | flops | bytes accessed | tf_op | source)
XLA Modules:
  0.0 646.8 jit_solution(5350321345478631937)
XLA Ops:
  8.8 12.0 %all-to-all-start = ((f32[32,256,16]{1,2,0:T(8,128)}), f32[32,256,16]{1,2,0:T(8,128)S(1)}, u32[]{:S(2)}, u32[]{:S(2)}) async-start(f32[32,256,16]{1,2,0:T(8,128)} %stack.2), calls=%async_computation | async-start | bytes 1048576 | tf_op jit(solution)/shard_map/all_to_all | solution.py:13
  22.3 39.4 %all_gather.10 = bf16[8192,32]{0,1:T(8,128)(2,1)S(1)} all-gather(bf16[256,32]{0,1:T(8,128)(2,1)S(1)} %multiply_convert_fusion), channel_id=1, replica_groups=mesh['row'=32,'col'=8] {'row'}, dimensions={0}, use_global_device_ids=true | all-gather | bytes 540672 | tf_op jit(solution)/shard_map/all_gather | solution.py:41
  63.5 22.6 %all_gather.9 = f32[2048,16]{0,1:T(8,128)S(1)} all-gather(f32[256,16]{0,1:T(8,128)S(1)} %broadcast_multiply_fusion), channel_id=1, replica_groups=mesh['row'=32,'col'=8] {'col'}, dimensions={0}, use_global_device_ids=true | all-gather | bytes 147456 | tf_op jit(solution)/shard_map/all_gather | solution.py:68
  87.0 107.7 %while.22 = (s32[]{:T(128)}, f32[2048,32]{0,1:T(8,128)S(1)}, f32[]{:T(128)}, f32[2048]{0:T(1024)S(1)}, f32[16,512]{1,0:T(8,128)S(1)}, /*index=5*/f32[16,512,16]{...) while((s32[]{:T(128)}, f32[2048,32]{0,1:T(8,128)S(1)}, ...), condition=%wide.region_5.6_spmd.clone, body=%wide.region_4.5_spmd.clone.sunk | while | flops 274857984 | bytes 5028475 | solution.py:51
  196.1 29.2 %reduce-scatter.3.cloned.1.call-done = f32[256,32]{0,1:T(8,128)} async-done(((f32[2048,32]{0,1:T(8,128)}), f32[256,32]{0,1:T(8,128)}) %reduce-scatter.3.cloned.1.call-update) | async-done | bytes 32784 | tf_op jit(solution)/shard_map/reduce_scatter | solution.py:83
  226.2 78.3 %all-reduce = (f32[32]{0:T(128)S(1)}, f32[32]{0:T(128)S(1)}) all-reduce(f32[32]{0:T(128)S(1)} %get-tuple-element.191, f32[32]{0:T(128)S(1)} %get-tuple-element.190), channel_id=1, replica_groups=mesh['row'=32,'col'=8] {'row','col'}, use_global_device_ids=true, to_apply=%region_1.0 | all-reduce | flops 64 | bytes 512 | tf_op jit(solution)/shard_map/psum | solution.py:34
  305.4 73.1 %psum.30 = f32[32]{0:T(128)S(1)} all-reduce(f32[32]{0:T(128)S(1)} %get-tuple-element.226), channel_id=1, replica_groups=mesh['row'=32,'col'=8] {'row','col'}, use_global_device_ids=true, to_apply=%region_10.11 | all-reduce | flops 32 | bytes 256 | tf_op jit(solution)/shard_map/psum | solution.py:34
  378.6 33.5 %all_gather.11 = bf16[8192,32]{0,1:T(8,128)(2,1)S(1)} all-gather(bf16[256,32]{0,1:T(8,128)(2,1)S(1)} %fusion.26), channel_id=1, replica_groups=mesh['row'=32,'col'=8] {'row'}, dimensions={0}, use_global_device_ids=true | all-gather | bytes 540672 | tf_op jit(solution)/shard_map/all_gather | solution.py:41
  413.9 107.7 %while.23 = (s32[]{:T(128)}, f32[2048,32]{0,1:T(8,128)S(1)}, f32[]{:T(128)}, f32[2048]{0:T(1024)S(1)}, f32[16,512]{1,0:T(8,128)S(1)}, /*index=5*/f32[16,512,16]{...) while((s32[]{:T(128)}, f32[2048,32]{0,1:T(8,128)S(1)}, ...), condition=%wide.region_12.13_spmd.clone, body=%wide.region_11.12_spmd.clone.sunk | while | flops 274857984 | bytes 5028475 | solution.py:51
  434.1 5.3 fusion.50
  440.8 5.3 fusion.50
  447.6 5.3 fusion.50
  454.3 5.3 fusion.50
  461.0 5.3 fusion.50
  467.8 5.3 fusion.50
  474.5 5.3 fusion.50
  481.2 5.3 fusion.50
  488.0 5.3 fusion.50
  494.7 5.3 fusion.50
  501.5 5.3 fusion.50
  508.2 5.3 fusion.50
  514.9 5.3 fusion.50
  522.4 37.1 %reduce-scatter.5.cloned.1.call-done = f32[256,32]{0,1:T(8,128)} async-done(((f32[2048,32]{0,1:T(8,128)}), f32[256,32]{0,1:T(8,128)}) %reduce-scatter.5.cloned.1.call-update) | async-done | bytes 32784 | tf_op jit(solution)/shard_map/reduce_scatter | solution.py:83
  560.3 78.2 %psum.31 = f32[32]{0:T(128)S(1)} all-reduce(f32[32]{0:T(128)S(1)} %fusion.21), channel_id=1, replica_groups=mesh['row'=32,'col'=8] {'row','col'}, use_global_device_ids=true, to_apply=%region_15.16 | all-reduce | flops 32 | bytes 256 | tf_op jit(solution)/shard_map/psum | solution.py:85
  (116 shorter events, 158.1 us)
Async XLA Ops:
  8.8 77.3 %all-to-all-start = ((f32[32,256,16]{1,2,0:T(8,128)}), f32[32,256,16]{1,2,0:T(8,128)S(1)}, u32[]{:S(2)}, u32[]{:S(2)}) async-start(f32[32,256,16]{1,2,0:T(8,128)} %stack.2), calls=%async_computation | async-start | bytes 1048576 | tf_op jit(solution)/shard_map/all_to_all | solution.py:13
  20.8 204.5 %reduce-scatter.3.cloned.1.call-start = ((), (), s32[]{:S(2)}) async-start(), calls=%async_computation.3 | async-start | bytes 294912 | tf_op jit(solution)/shard_map/reduce_scatter | solution.py:83
  87.0 138.3 %copy-start.2 = (f32[256,32]{0,1:T(8,128)S(1)}, f32[256,32]{0,1:T(8,128)}, u32[]{:S(2)}) copy-start(f32[256,32]{0,1:T(8,128)} %param.14) | copy-start | bytes 98308
  194.7 0.7 copy-start.1
  195.4 364.0 %reduce-scatter.5.cloned.1.call-start = ((), (), s32[]{:S(2)}) async-start(), calls=%async_computation.4 | async-start | bytes 294912 | tf_op jit(solution)/shard_map/reduce_scatter | solution.py:83
  521.6 0.7 copy-start
Sparse Core Ops, SparseCore 0:
  195.5 29.7 reduce-scatter.2
  522.5 36.8 reduce-scatter.4
